TPU v7x, 32 devices: a whole 2x2x4 slice. The times are simulated.
32 devices in a mesh: ctx: 8 (over z, y), tp: 4 (over x, core).
Axes of the slice: x: 2, y: 2, z: 4, core: 2. Of those that a mesh axis runs over, the one named last changes fastest.
Arguments:
- queries: bfloat16 [8192, 8192], P('ctx', 'tp'), may hold values from -170 to 170
- key_vectors: bfloat16 [8192, 8192], P('ctx', 'tp'), may hold values from -5 to 5
- value_vectors: bfloat16 [8192, 8192], P('ctx', 'tp'), may hold values from -5 to 5
- gate_logits: bfloat16 [8192, 8192], P('ctx', 'tp'), may hold values from -6 to 6
- norm_gain: float32 [8192], P('tp'), may hold values from 0.1 to 1.9
Outputs:
- attention_out: bfloat16 [8192, 8192], P('ctx', 'tp')
All inputs are finite; a program needn't handle non-finite values.
Results may differ from a plain program's by a relative error of at most 0.0028.
Values sent between devices are 32-bit elements; how exact they have to be, the bound alone decides.
A program may use at most 128 MiB of HBM per device.

v0:
```python
import jax
import jax.numpy as jnp
from jax import lax
from jax.sharding import PartitionSpec as P

HEADS = 64
HEAD_DIM = 128


def on_device(queries, key_vectors, value_vectors, gate_logits, norm_gain):
    rows = queries.shape[0]
    heads_local = queries.shape[1] // HEAD_DIM
    q_heads = queries.reshape(rows, heads_local, HEAD_DIM)
    k_heads = key_vectors.reshape(rows, heads_local, HEAD_DIM)
    v_heads = value_vectors.reshape(rows, heads_local, HEAD_DIM)
    state = jnp.einsum("shd,she->hde", k_heads, v_heads, preferred_element_type=jnp.float32)
    own_slab = lax.axis_index("ctx")
    piece = lax.all_gather(state[None], "ctx", axis=0, tiled=True)
    slab_ids = jnp.arange(piece.shape[0], dtype=jnp.int32)
    weights = (slab_ids < own_slab).astype(jnp.float32)
    prefix = jnp.sum(piece * weights[:, None, None, None], axis=0)
    places = jnp.arange(rows)
    causal = places[:, None] >= places[None, :]
    scores = jnp.einsum("qhd,khd->hqk", q_heads, k_heads, preferred_element_type=jnp.float32)
    scores = jnp.where(causal[None], scores, 0.0).astype(jnp.bfloat16)
    intra = jnp.einsum("hqk,khd->qhd", scores, v_heads, preferred_element_type=jnp.float32)
    inter = jnp.einsum(
        "qhd,hde->qhe", q_heads.astype(jnp.float32), prefix, precision=lax.Precision.HIGHEST
    )
    attn = (intra + inter).reshape(rows, heads_local * HEAD_DIM)
    local_squares = jnp.sum(attn * attn, axis=1)
    total_squares = lax.psum(local_squares, "tp")
    mean_square = total_squares / (HEADS * HEAD_DIM)
    result = (
        attn
        * lax.rsqrt(mean_square + 1e-05)[:, None]
        * norm_gain[None, :]
        * jax.nn.sigmoid(gate_logits.astype(jnp.float32))
    )
    return result.astype(jnp.bfloat16)


def solution(mesh):
    return jax.shard_map(
        on_device,
        mesh=mesh,
        in_specs=(P("ctx", "tp"), P("ctx", "tp"), P("ctx", "tp"), P("ctx", "tp"), P("tp")),
        out_specs=P("ctx", "tp"),
        check_vma=False,
    )
```

profile of v0, /device:TPU:0, one launch (start us, length us, event | category | flops | bytes accessed | tf_op | source)
XLA Modules:
  0.0 210.3 jit_solution(97442918351328215)
XLA Ops:
  6.5 0.0 all-gather.3.cloned.1.call-start
  6.5 6.4 %copy.18 = bf16[1024,2048]{0,1:T(8,128)(2,1)} copy(bf16[1024,2048]{1,0:T(8,128)(2,1)} %param.6) | data formatting | bytes 8388608 | tf_op jit(solution)/shard_map/reshape | solution.py:14
  12.9 5.9 %fusion.6 = f32[16,128,128]{2,1,0:T(8,128)} fusion(bf16[1024,16,128]{0,2,1:T(8,128)(2,1)} %bitcast.46, bf16[1024,2048]{1,0:T(8,128)(2,1)} %param.7), kind=kOutput, calls=%fused_computation.10 | convolution fusion | flops 536870912 | bytes 9437184 | tf_op jit(solution)/shard_map/shd,she->hde/dot_general | solution.py:16
  18.8 0.0 all-gather.3.cloned.1.call-update
  18.9 0.3 iota_compare_fusion
  19.2 127.0 %all-gather.3.cloned.1.call-done = f32[128,128,128]{2,1,0:T(8,128)} async-done(((f32[16,128,128]{2,1,0:T(8,128)}), f32[128,128,128]{2,1,0:T(8,128)}) %all-gather.3.cloned.1.call-update) | async-done | bytes 8388624 | tf_op jit(solution)/shard_map/all_gather | solution.py:18
  146.2 0.0 copy-start
  146.2 4.7 %multiply_reduce_fusion.1 = f32[16,128,128]{2,1,0:T(8,128)S(1)} fusion(f32[8,16,128,128]{3,2,1,0:T(8,128)} %bitcast.44, f32[8]{0:T(128)S(1)} %compare_convert_fusion), kind=kLoop, calls=%fused_computation.8 | loop fusion | flops 3932160 | bytes 9437216 | tf_op jit(solution)/shard_map/reduce_sum | solution.py:21
  150.9 0.0 copy-done
  151.0 5.9 %fusion.10 = f32[16,128,1024]{2,1,0:T(8,128)} fusion(f32[16,128,128]{2,1,0:T(8,128)S(1)} %multiply_reduce_fusion.1, bf16[1024,2048]{1,0:T(8,128)(2,1)S(1)} %copy-done), kind=kOutput, calls=%fused_computation.13 | convolution fusion | flops 3221225472 | bytes 13631488 | tf_op jit(solution)/shard_map/qhd,hde->qhe/dot_general | solution.py:27
  156.9 24.3 %multiply_reduce_fusion = (f32[1024]{0:T(1024)S(1)}, f32[1024,16,128]{0,2,1:T(8,128)}) fusion(f32[16,128,1024]{2,1,0:T(8,128)} %fusion.10, pred[1024,1024]{1,0:T(8,128)(4,1)S(1)} %iota_compare_fusion, bf16[1024,16,128]{0,2,1:T(8,128)(2,1)} %bitcast.47, bf16[1024,2048]{1,0:T(8,128)(2,1)} %param.7, bf16[1024,2048]{1,0:T(8,128)(2,1)} %param.5), kind=kOutput, calls=%fused_computation.7 | convolution fusion | flops 8629779456 | bytes 30412800 | tf_op jit(solution)/shard_map/hqk,khd->qhd/dot_general | solution.py:26
  181.2 5.8 %psum.7 = f32[1024]{0:T(1024)S(1)} all-reduce(f32[1024]{0:T(1024)S(1)} %get-tuple-element.5), channel_id=1, replica_groups=mesh['ctx'=8,'tp'=4] {'tp'}, use_global_device_ids=true, to_apply=%region_2.3 | all-reduce | flops 1024 | bytes 8192 | tf_op jit(solution)/shard_map/psum | solution.py:32
  187.0 0.0 copy-start.1
  187.0 9.2 %copy.16 = f32[1024,2048]{1,0:T(8,128)} copy(f32[1024,2048]{0,1:T(8,128)} %bitcast.45) | data formatting | bytes 16777216 | tf_op jit(solution)/shard_map/reshape | solution.py:30
  196.2 0.0 copy-done.1
  196.2 7.3 %multiply_convert_fusion = bf16[1024,2048]{1,0:T(8,128)(2,1)} fusion(bf16[1024,2048]{1,0:T(8,128)(2,1)} %param.8, f32[1024,2048]{1,0:T(8,128)} %copy.16, f32[2048]{0:T(1024)S(1)} %copy-done.1, f32[1024]{0:T(1024)S(1)} %add_rsqrt_fusion), kind=kLoop, calls=%fused_computation.6 | loop fusion | flops 16777216 | bytes 16789504 | tf_op jit(solution)/shard_map/convert_element_type | solution.py:40
  (2 shorter events, 0.0 us)
Async XLA Ops:
  6.5 139.7 %all-gather.3.cloned.1.call-start = ((), (), s32[]{:S(2)}) async-start(), calls=%async_computation | async-start | bytes 9437184 | tf_op jit(solution)/shard_map/all_gather | solution.py:18
  146.2 4.7 %copy-start = (bf16[1024,2048]{1,0:T(8,128)(2,1)S(1)}, bf16[1024,2048]{1,0:T(8,128)(2,1)}, u32[]{:S(2)}) copy-start(bf16[1024,2048]{1,0:T(8,128)(2,1)} %param.5) | copy-start | bytes 12582916
  187.0 9.2 %copy-start.1 = (f32[2048]{0:T(1024)S(1)}, f32[2048]{0:T(1024)}, u32[]{:S(2)}) copy-start(f32[2048]{0:T(1024)} %param.9) | copy-start | bytes 24580
Sparse Core Ops, SparseCore 0:
  19.0 127.1 all-gather.2
where the time goes:
time: 211 us; the launch traced here: 210 us
  waiting for transfers between devices  127 us (60%)
  matrix products  36.1 us (17%)
  local copies, waits for them, and re-layouts  15.6 us (7%)
  between operations  13.4 us (6%)
  other arithmetic  12.4 us (6%)
  blocking collectives  5.83 us (3%)
    all_gather x1, waiting for transfers between devices, on_device(): piece = lax.all_gather(state[None], 'ctx', axis=0, tiled=True)  127 us
    dot_general x1, matrix products, on_device(): jnp.einsum('hqk,khd->qhd', scores, v_heads, preferred_element_type=jnp.fl...  24.3 us
    reshape x1, local copies, waits for them, and re-layouts, on_device(): attn = (intra + inter).reshape(rows, heads_local * HEAD_DIM)  9.16 us
    convert_element_type x1, other arithmetic, on_device(): return result.astype(jnp.bfloat16)  7.32 us
    reshape x1, local copies, waits for them, and re-layouts, on_device(): k_heads = key_vectors.reshape(rows, heads_local, HEAD_DIM)  6.39 us
    dot_general x1, matrix products, on_device(): jnp.einsum('qhd,hde->qhe', q_heads.astype(jnp.float32), prefix, precision...  5.9 us
    dot_general x1, matrix products, on_device(): jnp.einsum('shd,she->hde', k_heads, v_heads, preferred_element_type=jnp.f...  5.9 us
    psum x1, blocking collectives, on_device(): total_squares = lax.psum(local_squares, 'tp')  5.83 us
  transfers between devices with their start and end apart: 1, of which 1 were waited for; matrix products, arithmetic and copies ran while one was open for 0% of the time, Pallas kernels for 0%

commit v1 on v0

v1 whole, which is shorter than its diff:
```python
import functools

import jax
import jax.numpy as jnp
from jax import lax
from jax.experimental import pallas as pl
from jax.experimental.pallas import tpu as pltpu
from jax.sharding import PartitionSpec as P

HEAD_DIM = 128
BLOCK = 256
STEPS_PER_HOP = 3
LAG = 3
MESH = pl.DeviceIdType.MESH


def columns_of(n_ctx):
    ny = 1
    while 2 * (2 * ny) * (2 * ny) <= n_ctx:
        ny *= 2
    return ny


def attention_kernel(
    n_ctx, n_tp,
    q_hbm, k_hbm, v_hbm, g_hbm, gain_ref,
    gated_hbm, scale_ref,
    q_buf, k_buf, v_buf, g_buf, attn, state,
    z_in, z_out, f_in, f_out, b_in, b_out,
    squares, sums, sums_in,
    load_sem, store_sem, z_send, z_recv, f_send, f_recv, b_send, b_recv, s_send, s_recv,
):
    heads, rows, _ = q_buf.shape
    ny = columns_of(n_ctx)
    nz = n_ctx // ny
    ctx = lax.axis_index("ctx")
    tp = lax.axis_index("tp")
    z = ctx // ny
    y = lax.rem(ctx, ny)

    def load(which, hbm, buf, h):
        return pltpu.make_async_copy(
            hbm.at[:, pl.ds(pl.multiple_of(h * HEAD_DIM, HEAD_DIM), HEAD_DIM)],
            buf.at[h], load_sem.at[which, h])

    def store(h):
        return pltpu.make_async_copy(
            attn.at[h],
            gated_hbm.at[:, pl.ds(pl.multiple_of(h * HEAD_DIM, HEAD_DIM), HEAD_DIM)],
            store_sem.at[h])

    def send(src, dst, ssem, rsem, h, to):
        return pltpu.make_async_remote_copy(
            src_ref=src.at[h], dst_ref=dst.at[h], send_sem=ssem.at[h], recv_sem=rsem.at[h],
            device_id=(to, tp), device_id_type=MESH)

    z_copy = lambda h: send(z_out, z_in, z_send, z_recv, h, jnp.minimum(ctx + ny, n_ctx - 1))
    f_copy = lambda h: send(f_out, f_in, f_send, f_recv, h, jnp.minimum(ctx + 1, n_ctx - 1))
    b_copy = lambda h: send(b_out, b_in, b_send, b_recv, h, jnp.maximum(ctx - 1, 0))

    def sum_copy(d):
        return pltpu.make_async_remote_copy(
            src_ref=sums, dst_ref=sums_in.at[d - 1], send_sem=s_send.at[d - 1],
            recv_sem=s_recv.at[d - 1], device_id=(ctx, lax.rem(tp + d, n_tp)),
            device_id_type=MESH)

    @pl.loop(0, heads)
    def _(h):
        load(0, k_hbm, k_buf, h).start()
        load(1, v_hbm, v_buf, h).start()

    @pl.loop(0, heads)
    def _(h):
        load(2, q_hbm, q_buf, h).start()
        load(3, g_hbm, g_buf, h).start()

    up, down, right, left = z < nz - 1, z > 0, y < ny - 1, y > 0
    barrier = pltpu.get_barrier_semaphore()
    for there, step in ((up, ny), (down, -ny), (right, 1), (left, -1)):
        @pl.when(there)
        def _():
            pl.semaphore_signal(barrier, inc=1, device_id=(ctx + step, tp), device_id_type=MESH)
    for d in range(1, n_tp):
        pl.semaphore_signal(
            barrier, inc=1, device_id=(ctx, lax.rem(tp + d, n_tp)), device_id_type=MESH)
    greeted = n_tp - 1
    for there in (up, down, right, left):
        greeted = greeted + jnp.where(there, 1, 0)
    pl.semaphore_wait(barrier, greeted)

    squares[...] = jnp.zeros_like(squares)

    def relay(h):
        @pl.when(down)
        def _():
            z_copy(h).wait_recv()

        @pl.when(z == 0)
        def _():
            z_in[h] = jnp.zeros((HEAD_DIM, HEAD_DIM), jnp.float32)

        before = z_in[h]
        after = before + state[h]

        @pl.when(up)
        def _():
            z_out[h] = after
            z_copy(h).start()

        @pl.when(jnp.logical_and(right, y == 0))
        def _():
            f_out[h] = after
            f_copy(h).start()

        @pl.when(jnp.logical_and(left, y == ny - 1))
        def _():
            b_out[h] = before
            b_copy(h).start()

    def finalize(h):
        prefix_in = z_in[h]
        zeros = jnp.zeros((HEAD_DIM, HEAD_DIM), jnp.float32)

        @pl.when(left)
        def _():
            f_copy(h).wait_recv()

            @pl.when(right)
            def _():
                f_out[h] = f_in[h] + (prefix_in + state[h])
                f_copy(h).start()

        @pl.when(y == 0)
        def _():
            f_in[h] = zeros

        @pl.when(right)
        def _():
            b_copy(h).wait_recv()

            @pl.when(left)
            def _():
                b_out[h] = b_in[h] + prefix_in
                b_copy(h).start()

        @pl.when(y == ny - 1)
        def _():
            b_in[h] = zeros

        prefix = prefix_in + f_in[h] + b_in[h]
        high = prefix.astype(jnp.bfloat16)
        low = (prefix - high.astype(jnp.float32)).astype(jnp.bfloat16)
        both = jnp.concatenate([high, low], axis=1)
        load(3, g_hbm, g_buf, h).wait()
        gain = gain_ref[h]
        for i in range(rows // BLOCK):
            here = pl.ds(i * BLOCK, BLOCK)
            inter = jnp.dot(q_buf[h, here, :], both, preferred_element_type=jnp.float32)
            total = attn[h, here, :] + (inter[:, :HEAD_DIM] + inter[:, HEAD_DIM:])
            squares[here, :] += total * total
            gate = jax.nn.sigmoid(g_buf[h, here, :].astype(jnp.float32))
            attn[h, here, :] = total * gain * gate
        store(h).start()

    def intra(h):
        load(2, q_hbm, q_buf, h).wait()
        row = lax.broadcasted_iota(jnp.int32, (BLOCK, BLOCK), 0)
        column = lax.broadcasted_iota(jnp.int32, (BLOCK, BLOCK), 1)
        for i in range(rows // BLOCK):
            here = pl.ds(i * BLOCK, BLOCK)
            q = q_buf[h, here, :]
            own = lax.dot_general(
                q, k_buf[h, here, :], (((1,), (1,)), ((), ())), preferred_element_type=jnp.float32)
            own = jnp.where(row >= column, own, 0.0).astype(jnp.bfloat16)
            out = jnp.dot(own, v_buf[h, here, :], preferred_element_type=jnp.float32)
            if i > 0:
                past = pl.ds(0, i * BLOCK)
                scores = lax.dot_general(
                    q, k_buf[h, past, :], (((1,), (1,)), ((), ())),
                    preferred_element_type=jnp.float32).astype(jnp.bfloat16)
                out += jnp.dot(scores, v_buf[h, past, :], preferred_element_type=jnp.float32)
            attn[h, here, :] = out

    @pl.loop(0, heads)
    def _(h):
        load(0, k_hbm, k_buf, h).wait()
        load(1, v_hbm, v_buf, h).wait()
        state[h] = lax.dot_general(
            k_buf[h], v_buf[h], (((0,), (0,)), ((), ())), preferred_element_type=jnp.float32)

        @pl.when(z == 0)
        def _():
            relay(h)

    delay = z * STEPS_PER_HOP

    @pl.loop(0, heads + delay + LAG)
    def _(s):
        @pl.when(jnp.logical_and(z > 0, jnp.logical_and(s >= delay, s < delay + heads)))
        def _():
            relay(s - delay)

        @pl.when(s < heads)
        def _():
            intra(s)

        @pl.when(s >= delay + LAG)
        def _():
            finalize(s - delay - LAG)

    sums[...] = jnp.sum(jnp.transpose(squares[...]), axis=0, keepdims=True)
    for d in range(1, n_tp):
        sum_copy(d).start()
    total = sums[...]
    for d in range(1, n_tp):
        sum_copy(d).wait_recv()
        total = total + sums_in[d - 1]
    mean_square = total / (heads * HEAD_DIM * n_tp)
    scale = lax.rsqrt(mean_square + 1e-05)
    scale_ref[...] = jnp.transpose(jnp.broadcast_to(scale, (HEAD_DIM, rows)))

    for d in range(1, n_tp):
        sum_copy(d).wait_send()

    @pl.loop(0, heads)
    def _(h):
        store(h).wait()

        @pl.when(up)
        def _():
            z_copy(h).wait_send()

        @pl.when(right)
        def _():
            f_copy(h).wait_send()

        @pl.when(left)
        def _():
            b_copy(h).wait_send()


def norm_kernel(gated_ref, scale_ref, out_ref):
    scale = scale_ref[...]
    for h in range(gated_ref.shape[1] // HEAD_DIM):
        here = pl.ds(h * HEAD_DIM, HEAD_DIM)
        out_ref[:, here] = (gated_ref[:, here] * scale).astype(out_ref.dtype)


def on_device(n_ctx, n_tp, queries, key_vectors, value_vectors, gate_logits, norm_gain):
    rows, width = queries.shape
    heads = width // HEAD_DIM
    head_array = lambda dtype: pltpu.VMEM((heads, rows, HEAD_DIM), dtype)
    states = pltpu.VMEM((heads, HEAD_DIM, HEAD_DIM), jnp.float32)
    dma = pltpu.SemaphoreType.DMA
    hbm = pl.BlockSpec(memory_space=pl.ANY)
    vmem = pl.BlockSpec(memory_space=pltpu.VMEM)
    gated, scale = pl.pallas_call(
        functools.partial(attention_kernel, n_ctx, n_tp),
        out_shape=(
            jax.ShapeDtypeStruct((rows, width), jnp.float32),
            jax.ShapeDtypeStruct((rows, HEAD_DIM), jnp.float32),
        ),
        in_specs=[hbm, hbm, hbm, hbm, vmem],
        out_specs=(hbm, vmem),
        scratch_shapes=[
            head_array(jnp.bfloat16), head_array(jnp.bfloat16), head_array(jnp.bfloat16),
            head_array(jnp.bfloat16), head_array(jnp.float32),
            states, states, states, states, states, states, states,
            pltpu.VMEM((rows, HEAD_DIM), jnp.float32),
            pltpu.VMEM((1, rows), jnp.float32),
            pltpu.VMEM((n_tp - 1, 1, rows), jnp.float32),
            dma((4, heads)), dma((heads,)),
            dma((heads,)), dma((heads,)), dma((heads,)), dma((heads,)), dma((heads,)), dma((heads,)),
            dma((n_tp - 1,)), dma((n_tp - 1,)),
        ],
        compiler_params=pltpu.CompilerParams(
            collective_id=0, has_side_effects=True, vmem_limit_bytes=48 * 1024 * 1024),
        name="attention",
    )(queries, key_vectors, value_vectors, gate_logits, norm_gain.reshape(heads, 1, HEAD_DIM))
    tile = min(rows, 128)
    return pl.pallas_call(
        norm_kernel,
        grid=(rows // tile,),
        out_shape=jax.ShapeDtypeStruct((rows, width), jnp.bfloat16),
        in_specs=[
            pl.BlockSpec((tile, width), lambda i: (i, 0)),
            pl.BlockSpec((tile, HEAD_DIM), lambda i: (i, 0)),
        ],
        out_specs=pl.BlockSpec((tile, width), lambda i: (i, 0)),
        name="norm",
    )(gated, scale)


def solution(mesh):
    return jax.shard_map(
        functools.partial(on_device, mesh.shape["ctx"], mesh.shape["tp"]),
        mesh=mesh,
        in_specs=(P("ctx", "tp"), P("ctx", "tp"), P("ctx", "tp"), P("ctx", "tp"), P("tp")),
        out_specs=P("ctx", "tp"),
        check_vma=False,
    )
```

time: 211 us -> 59.6 us (0.28)
  the two profiles are of different devices: /device:TPU:0 before, /device:TPU:25 now
where the time goes in v1:
time: 59.6 us; the launch traced here: 59.2 us
  Pallas kernels  55.5 us (93%)
  local copies, waits for them, and re-layouts  3.71 us (6%)
    pallas_call x1, Pallas kernels, on_device(): pl.pallas_call(functools.partial(attention_kernel, n_ctx, n_tp), out_shap...  47.5 us
    pallas_call x1, Pallas kernels, on_device(): pl.pallas_call(norm_kernel, grid=(rows // tile,), out_shape=jax.ShapeDtyp...  7.94 us
    unnamed x6, local copies, waits for them, and re-layouts  3.71 us

profile of v1, /device:TPU:25, one launch (start us, length us, event | category | flops | bytes accessed | tf_op | source)
XLA Modules:
  0.0 59.2 jit_solution(7387472355042189202)
XLA Ops:
  0.0 0.0 copy-start
  0.0 2.2 %copy-done = bf16[1024,2048]{1,0:T(8,128)(2,1)S(1)} copy-done((bf16[1024,2048]{1,0:T(8,128)(2,1)S(1)}, bf16[1024,2048]{1,0:T(8,128)(2,1)}, u32[]{:S(2)}) %copy-start) | copy-done | bytes 4194328
  2.2 0.0 copy-start.2
  2.2 0.7 %copy-done.2 = f32[2048]{0:T(1024)S(1)} copy-done((f32[2048]{0:T(1024)S(1)}, f32[2048]{0:T(1024)}, u32[]{:S(2)}) %copy-start.2) | copy-done | bytes 8216
  2.9 47.5 %attention.1 = (f32[1024,2048]{1,0:T(8,128)}, f32[1024,128]{1,0:T(8,128)S(1)}) custom-call(bf16[1024,2048]{1,0:T(8,128)(2,1)S(1)} %copy-done, bf16[1024,2048]{1,0:T(8,128)(2,1)} %k_hbm.1, bf16[1024,2048]{1,0:T(8,128)(2,1)} %v_hbm.1, bf16[1024,2048]{1,0:T(8,128)(2,1)} %g_hbm.1, f32[16,1,128]{2,1,0:T(1,128)S(1)} %bitcast.1), custom_call_target="tpu_custom_call" | custom-call | tf_op jit(solution)/shard_map/attention/pallas_call | solution.py:257
  50.4 0.0 copy-start.1
  50.4 0.8 %copy-done.1 = f32[1024,128]{1,0:T(8,128)} copy-done((f32[1024,128]{1,0:T(8,128)}, f32[1024,128]{1,0:T(8,128)S(1)}, u32[]{:S(2)}) %copy-start.1) | copy-done | bytes 524312
  51.3 7.9 %norm.1 = bf16[1024,2048]{1,0:T(8,128)(2,1)} custom-call(f32[1024,2048]{1,0:T(8,128)} %get-tuple-element.7.gated_ref, f32[1024,128]{1,0:T(8,128)} %copy-done.1), custom_call_target="tpu_custom_call" | custom-call | tf_op jit(solution)/shard_map/norm/pallas_call | solution.py:281
Async XLA Ops:
  0.0 2.2 %copy-start = (bf16[1024,2048]{1,0:T(8,128)(2,1)S(1)}, bf16[1024,2048]{1,0:T(8,128)(2,1)}, u32[]{:S(2)}) copy-start(bf16[1024,2048]{1,0:T(8,128)(2,1)} %q_hbm.1) | copy-start | bytes 12582916
  2.2 0.7 %copy-start.2 = (f32[2048]{0:T(1024)S(1)}, f32[2048]{0:T(1024)}, u32[]{:S(2)}) copy-start(f32[2048]{0:T(1024)} %param.9) | copy-start | bytes 24580
  50.4 0.8 %copy-start.1 = (f32[1024,128]{1,0:T(8,128)}, f32[1024,128]{1,0:T(8,128)S(1)}, u32[]{:S(2)}) copy-start(f32[1024,128]{1,0:T(8,128)S(1)} %get-tuple-element.8.scale_ref) | copy-start | bytes 1572868

commit v2 on v1

--- a/solution.py
+++ b/solution.py
@@ -11,6 +11,7 @@
 BLOCK = 256
 STEPS_PER_HOP = 3
 LAG = 3
+NORM_ROWS = 128
 MESH = pl.DeviceIdType.MESH
 
 
@@ -23,14 +24,15 @@
 
 def attention_kernel(
     n_ctx, n_tp,
-    q_hbm, k_hbm, v_hbm, g_hbm, gain_ref,
-    gated_hbm, scale_ref,
-    q_buf, k_buf, v_buf, g_buf, attn, state,
+    q_hbm, k_hbm, v_hbm, g_hbm, gain_hbm,
+    attn, scale_ref,
+    q_buf, k_buf, v_buf, g_buf, gain_ref, states,
     z_in, z_out, f_in, f_out, b_in, b_out,
     squares, sums, sums_in,
-    load_sem, store_sem, z_send, z_recv, f_send, f_recv, b_send, b_recv, s_send, s_recv,
+    load_sem, gain_sem, z_send, z_recv, f_send, f_recv, b_send, b_recv, s_send, s_recv,
 ):
     heads, rows, _ = q_buf.shape
+    blocks = rows // BLOCK
     ny = columns_of(n_ctx)
     nz = n_ctx // ny
     ctx = lax.axis_index("ctx")
@@ -43,12 +45,6 @@
             hbm.at[:, pl.ds(pl.multiple_of(h * HEAD_DIM, HEAD_DIM), HEAD_DIM)],
             buf.at[h], load_sem.at[which, h])
 
-    def store(h):
-        return pltpu.make_async_copy(
-            attn.at[h],
-            gated_hbm.at[:, pl.ds(pl.multiple_of(h * HEAD_DIM, HEAD_DIM), HEAD_DIM)],
-            store_sem.at[h])
-
     def send(src, dst, ssem, rsem, h, to):
         return pltpu.make_async_remote_copy(
             src_ref=src.at[h], dst_ref=dst.at[h], send_sem=ssem.at[h], recv_sem=rsem.at[h],
@@ -73,6 +69,8 @@
     def _(h):
         load(2, q_hbm, q_buf, h).start()
         load(3, g_hbm, g_buf, h).start()
+
+    pltpu.make_async_copy(gain_hbm, gain_ref, gain_sem).start()
 
     up, down, right, left = z < nz - 1, z > 0, y < ny - 1, y > 0
     barrier = pltpu.get_barrier_semaphore()
@@ -100,7 +98,7 @@
             z_in[h] = jnp.zeros((HEAD_DIM, HEAD_DIM), jnp.float32)
 
         before = z_in[h]
-        after = before + state[h]
+        after = before + states[h, blocks - 1]
 
         @pl.when(up)
         def _():
@@ -127,7 +125,7 @@
 
             @pl.when(right)
             def _():
-                f_out[h] = f_in[h] + (prefix_in + state[h])
+                f_out[h] = f_in[h] + (prefix_in + states[h, blocks - 1])
                 f_copy(h).start()
 
         @pl.when(y == 0)
@@ -148,50 +146,50 @@
             b_in[h] = zeros
 
         prefix = prefix_in + f_in[h] + b_in[h]
-        high = prefix.astype(jnp.bfloat16)
-        low = (prefix - high.astype(jnp.float32)).astype(jnp.bfloat16)
-        both = jnp.concatenate([high, low], axis=1)
         load(3, g_hbm, g_buf, h).wait()
         gain = gain_ref[h]
-        for i in range(rows // BLOCK):
+        for i in range(blocks):
             here = pl.ds(i * BLOCK, BLOCK)
+            before = prefix if i == 0 else prefix + states[h, i - 1]
+            high = before.astype(jnp.bfloat16)
+            low = (before - high.astype(jnp.float32)).astype(jnp.bfloat16)
+            both = jnp.concatenate([high, low], axis=1)
             inter = jnp.dot(q_buf[h, here, :], both, preferred_element_type=jnp.float32)
             total = attn[h, here, :] + (inter[:, :HEAD_DIM] + inter[:, HEAD_DIM:])
             squares[here, :] += total * total
-            gate = jax.nn.sigmoid(g_buf[h, here, :].astype(jnp.float32))
+            gate = 0.5 + 0.5 * jnp.tanh(0.5 * g_buf[h, here, :].astype(jnp.float32))
             attn[h, here, :] = total * gain * gate
-        store(h).start()
 
     def intra(h):
         load(2, q_hbm, q_buf, h).wait()
         row = lax.broadcasted_iota(jnp.int32, (BLOCK, BLOCK), 0)
         column = lax.broadcasted_iota(jnp.int32, (BLOCK, BLOCK), 1)
-        for i in range(rows // BLOCK):
+        for i in range(blocks):
             here = pl.ds(i * BLOCK, BLOCK)
             q = q_buf[h, here, :]
             own = lax.dot_general(
                 q, k_buf[h, here, :], (((1,), (1,)), ((), ())), preferred_element_type=jnp.float32)
             own = jnp.where(row >= column, own, 0.0).astype(jnp.bfloat16)
-            out = jnp.dot(own, v_buf[h, here, :], preferred_element_type=jnp.float32)
-            if i > 0:
-                past = pl.ds(0, i * BLOCK)
-                scores = lax.dot_general(
-                    q, k_buf[h, past, :], (((1,), (1,)), ((), ())),
-                    preferred_element_type=jnp.float32).astype(jnp.bfloat16)
-                out += jnp.dot(scores, v_buf[h, past, :], preferred_element_type=jnp.float32)
-            attn[h, here, :] = out
+            attn[h, here, :] = jnp.dot(own, v_buf[h, here, :], preferred_element_type=jnp.float32)
 
     @pl.loop(0, heads)
     def _(h):
         load(0, k_hbm, k_buf, h).wait()
         load(1, v_hbm, v_buf, h).wait()
-        state[h] = lax.dot_general(
-            k_buf[h], v_buf[h], (((0,), (0,)), ((), ())), preferred_element_type=jnp.float32)
+        running = None
+        for i in range(blocks):
+            here = pl.ds(i * BLOCK, BLOCK)
+            own = lax.dot_general(
+                k_buf[h, here, :], v_buf[h, here, :], (((0,), (0,)), ((), ())),
+                preferred_element_type=jnp.float32)
+            running = own if i == 0 else running + own
+            states[h, i] = running
 
         @pl.when(z == 0)
         def _():
             relay(h)
 
+    pltpu.make_async_copy(gain_hbm, gain_ref, gain_sem).wait()
     delay = z * STEPS_PER_HOP
 
     @pl.loop(0, heads + delay + LAG)
@@ -224,8 +222,6 @@
 
     @pl.loop(0, heads)
     def _(h):
-        store(h).wait()
-
         @pl.when(up)
         def _():
             z_copy(h).wait_send()
@@ -239,11 +235,23 @@
             b_copy(h).wait_send()
 
 
-def norm_kernel(gated_ref, scale_ref, out_ref):
-    scale = scale_ref[...]
-    for h in range(gated_ref.shape[1] // HEAD_DIM):
-        here = pl.ds(h * HEAD_DIM, HEAD_DIM)
-        out_ref[:, here] = (gated_ref[:, here] * scale).astype(out_ref.dtype)
+def norm_kernel(gated_ref, scale_ref, out_hbm, tiles, sems):
+    heads, rows, _ = gated_ref.shape
+    count = rows // NORM_ROWS
+
+    def store(i):
+        here = pl.ds(i * NORM_ROWS, NORM_ROWS)
+        return pltpu.make_async_copy(tiles.at[here, :], out_hbm.at[here, :], sems.at[i])
+
+    for i in range(count):
+        here = pl.ds(i * NORM_ROWS, NORM_ROWS)
+        scale = scale_ref[here, :]
+        for h in range(heads):
+            tiles[here, pl.ds(h * HEAD_DIM, HEAD_DIM)] = (
+                gated_ref[h, here, :] * scale).astype(tiles.dtype)
+        store(i).start()
+    for i in range(count):
+        store(i).wait()
 
 
 def on_device(n_ctx, n_tp, queries, key_vectors, value_vectors, gate_logits, norm_gain):
@@ -252,41 +260,39 @@
     head_array = lambda dtype: pltpu.VMEM((heads, rows, HEAD_DIM), dtype)
     states = pltpu.VMEM((heads, HEAD_DIM, HEAD_DIM), jnp.float32)
     dma = pltpu.SemaphoreType.DMA
-    hbm = pl.BlockSpec(memory_space=pl.ANY)
+    hbm = pl.BlockSpec(memory_space=pltpu.HBM)
     vmem = pl.BlockSpec(memory_space=pltpu.VMEM)
     gated, scale = pl.pallas_call(
         functools.partial(attention_kernel, n_ctx, n_tp),
         out_shape=(
-            jax.ShapeDtypeStruct((rows, width), jnp.float32),
-            jax.ShapeDtypeStruct((rows, HEAD_DIM), jnp.float32),
+            pltpu.VMEM((heads, rows, HEAD_DIM), jnp.float32),
+            pltpu.VMEM((rows, HEAD_DIM), jnp.float32),
         ),
-        in_specs=[hbm, hbm, hbm, hbm, vmem],
-        out_specs=(hbm, vmem),
+        in_specs=[hbm, hbm, hbm, hbm, hbm],
+        out_specs=(vmem, vmem),
         scratch_shapes=[
             head_array(jnp.bfloat16), head_array(jnp.bfloat16), head_array(jnp.bfloat16),
-            head_array(jnp.bfloat16), head_array(jnp.float32),
-            states, states, states, states, states, states, states,
+            head_array(jnp.bfloat16), pltpu.VMEM((heads, 1, HEAD_DIM), jnp.float32),
+            pltpu.VMEM((heads, rows // BLOCK, HEAD_DIM, HEAD_DIM), jnp.float32),
+            states, states, states, states, states, states,
             pltpu.VMEM((rows, HEAD_DIM), jnp.float32),
             pltpu.VMEM((1, rows), jnp.float32),
             pltpu.VMEM((n_tp - 1, 1, rows), jnp.float32),
-            dma((4, heads)), dma((heads,)),
+            dma((4, heads)), dma(()),
             dma((heads,)), dma((heads,)), dma((heads,)), dma((heads,)), dma((heads,)), dma((heads,)),
             dma((n_tp - 1,)), dma((n_tp - 1,)),
         ],
         compiler_params=pltpu.CompilerParams(
-            collective_id=0, has_side_effects=True, vmem_limit_bytes=48 * 1024 * 1024),
+            collective_id=0, has_side_effects=True, vmem_limit_bytes=50 * 1024 * 1024),
         name="attention",
     )(queries, key_vectors, value_vectors, gate_logits, norm_gain.reshape(heads, 1, HEAD_DIM))
-    tile = min(rows, 128)
     return pl.pallas_call(
         norm_kernel,
-        grid=(rows // tile,),
         out_shape=jax.ShapeDtypeStruct((rows, width), jnp.bfloat16),
-        in_specs=[
-            pl.BlockSpec((tile, width), lambda i: (i, 0)),
-            pl.BlockSpec((tile, HEAD_DIM), lambda i: (i, 0)),
-        ],
-        out_specs=pl.BlockSpec((tile, width), lambda i: (i, 0)),
+        in_specs=[vmem, vmem],
+        out_specs=hbm,
+        scratch_shapes=[pltpu.VMEM((rows, width), jnp.bfloat16), dma((rows // NORM_ROWS,))],
+        compiler_params=pltpu.CompilerParams(vmem_limit_bytes=16 * 1024 * 1024),
         name="norm",
     )(gated, scale)
 

time: 59.6 us -> 46.9 us (0.79)
  Pallas kernels: 55.5 us -> 46.8 us
  local copies, waits for them, and re-layouts: 3.71 us -> 0 us
    pallas_call x1, Pallas kernels: 7.94 us -> 2.2 us  [on_device(): pl.pallas_call(norm_kernel, out_shape=jax.ShapeDtypeStruct((rows, width),...]
    unnamed x6 -> x0, local copies, waits for them, and re-layouts: 3.71 us -> none
    pallas_call x1, Pallas kernels: 47.5 us -> 44.6 us  [on_device(): pl.pallas_call(functools.partial(attention_kernel, n_ctx, n_tp), out_shap...]
where the time goes in v2:
time: 46.9 us; the launch traced here: 46.8 us
  Pallas kernels  46.8 us (100%)
    pallas_call x1, Pallas kernels, on_device(): pl.pallas_call(functools.partial(attention_kernel, n_ctx, n_tp), out_shap...  44.6 us
    pallas_call x1, Pallas kernels, on_device(): pl.pallas_call(norm_kernel, out_shape=jax.ShapeDtypeStruct((rows, width),...  2.2 us

profile of v2, /device:TPU:25, one launch (start us, length us, event | category | flops | bytes accessed | tf_op | source)
XLA Modules:
  0.0 46.8 jit_solution(913596648120430308)
XLA Ops:
  0.0 44.6 %attention.1 = (f32[16,1024,128]{2,1,0:T(8,128)S(1)}, f32[1024,128]{1,0:T(8,128)S(1)}) custom-call(bf16[1024,2048]{1,0:T(8,128)(2,1)} %q_hbm.1, bf16[1024,2048]{1,0:T(8,128)(2,1)} %k_hbm.1, bf16[1024,2048]{1,0:T(8,128)(2,1)} %v_hbm.1, bf16[1024,2048]{1,0:T(8,128)(2,1)} %g_hbm.1, f32[16,1,128]{2,1,0:T(1,128)} %bitcast.1), custom_call_target="tpu_custom_call" | custom-call | tf_op jit(solution)/shard_map/attention/pallas_call | solution.py:265
  44.6 2.2 %norm.1 = bf16[1024,2048]{1,0:T(8,128)(2,1)} custom-call(f32[16,1024,128]{2,1,0:T(8,128)S(1)} %get-tuple-element.7.gated_ref, f32[1024,128]{1,0:T(8,128)S(1)} %get-tuple-element.8.scale_ref), custom_call_target="tpu_custom_call" | custom-call | tf_op jit(solution)/shard_map/norm/pallas_call | solution.py:289

commit v3 on v2

--- a/solution.py
+++ b/solution.py
@@ -9,8 +9,10 @@
 
 HEAD_DIM = 128
 BLOCK = 256
-STEPS_PER_HOP = 3
+STEPS_PER_HOP = 4
 LAG = 3
+FIRST_RELAY = 2
+OWN_LAG = 4
 NORM_ROWS = 128
 MESH = pl.DeviceIdType.MESH
 
@@ -60,13 +62,17 @@
             recv_sem=s_recv.at[d - 1], device_id=(ctx, lax.rem(tp + d, n_tp)),
             device_id_type=MESH)
 
+    first = heads // 2 * (1 - y) if ny == 2 else 0
+
     @pl.loop(0, heads)
-    def _(h):
+    def _(i):
+        h = lax.rem(i + first, heads)
         load(0, k_hbm, k_buf, h).start()
         load(1, v_hbm, v_buf, h).start()
 
     @pl.loop(0, heads)
-    def _(h):
+    def _(i):
+        h = lax.rem(i + first, heads)
         load(2, q_hbm, q_buf, h).start()
         load(3, g_hbm, g_buf, h).start()
 
@@ -146,6 +152,9 @@
             b_in[h] = zeros
 
         prefix = prefix_in + f_in[h] + b_in[h]
+        apply_prefix(h, prefix)
+
+    def apply_prefix(h, prefix):
         load(3, g_hbm, g_buf, h).wait()
         gain = gain_ref[h]
         for i in range(blocks):
@@ -164,16 +173,22 @@
         load(2, q_hbm, q_buf, h).wait()
         row = lax.broadcasted_iota(jnp.int32, (BLOCK, BLOCK), 0)
         column = lax.broadcasted_iota(jnp.int32, (BLOCK, BLOCK), 1)
-        for i in range(blocks):
-            here = pl.ds(i * BLOCK, BLOCK)
-            q = q_buf[h, here, :]
-            own = lax.dot_general(
-                q, k_buf[h, here, :], (((1,), (1,)), ((), ())), preferred_element_type=jnp.float32)
-            own = jnp.where(row >= column, own, 0.0).astype(jnp.bfloat16)
-            attn[h, here, :] = jnp.dot(own, v_buf[h, here, :], preferred_element_type=jnp.float32)
-
-    @pl.loop(0, heads)
-    def _(h):
+        places = [pl.ds(i * BLOCK, BLOCK) for i in range(blocks)]
+        scores = [
+            lax.dot_general(
+                q_buf[h, here, :], k_buf[h, here, :], (((1,), (1,)), ((), ())),
+                preferred_element_type=jnp.float32)
+            for here in places
+        ]
+        scores = [jnp.where(row >= column, own, 0.0).astype(jnp.bfloat16) for own in scores]
+        outs = [
+            jnp.dot(own, v_buf[h, here, :], preferred_element_type=jnp.float32)
+            for own, here in zip(scores, places)
+        ]
+        for here, out in zip(places, outs):
+            attn[h, here, :] = out
+
+    def slab_state(h):
         load(0, k_hbm, k_buf, h).wait()
         load(1, v_hbm, v_buf, h).wait()
         running = None
@@ -185,26 +200,128 @@
             running = own if i == 0 else running + own
             states[h, i] = running
 
+    def run_chains():
+        @pl.loop(0, heads)
+        def _(h):
+            slab_state(h)
+
+            @pl.when(z == 0)
+            def _():
+                relay(h)
+
+        delay = z * STEPS_PER_HOP
+
+        @pl.loop(0, heads + delay + LAG)
+        def _(s):
+            @pl.when(jnp.logical_and(z > 0, jnp.logical_and(s >= delay, s < delay + heads)))
+            def _():
+                relay(s - delay)
+
+            @pl.when(s < heads)
+            def _():
+                intra(s)
+
+            @pl.when(s >= delay + LAG)
+            def _():
+                finalize(s - delay - LAG)
+
+        @pl.loop(0, heads)
+        def _(h):
+            @pl.when(up)
+            def _():
+                z_copy(h).wait_send()
+
+            @pl.when(right)
+            def _():
+                f_copy(h).wait_send()
+
+            @pl.when(left)
+            def _():
+                b_copy(h).wait_send()
+
+    half = heads // 2
+    mate = ctx + 1 - 2 * y
+
+    def raw_copy(i):
+        return pltpu.make_async_remote_copy(
+            src_ref=states.at[(1 - y) * half + i, blocks - 1], dst_ref=f_in.at[i],
+            send_sem=f_send.at[i], recv_sem=f_recv.at[i],
+            device_id=(mate, tp), device_id_type=MESH)
+
+    mate_copy = lambda i: send(b_out, b_in, b_send, b_recv, i, mate)
+
+    def pair_relay(i):
+        h = y * half + i
+        raw_copy(i).wait_recv()
+
+        @pl.when(down)
+        def _():
+            z_copy(i).wait_recv()
+
         @pl.when(z == 0)
         def _():
-            relay(h)
+            z_in[i] = jnp.zeros((HEAD_DIM, HEAD_DIM), jnp.float32)
+
+        before = z_in[i]
+        mine = states[h, blocks - 1]
+
+        @pl.when(up)
+        def _():
+            z_out[i] = before + (mine + f_in[i])
+            z_copy(i).start()
+
+        b_out[i] = before + jnp.where(y == 0, mine, 0.0)
+        mate_copy(i).start()
+
+    def run_pairs():
+        @pl.loop(0, half)
+        def _(i):
+            slab_state((1 - y) * half + i)
+            raw_copy(i).start()
+
+        @pl.loop(0, half)
+        def _(i):
+            slab_state(y * half + i)
+
+        delay = FIRST_RELAY + z * STEPS_PER_HOP
+
+        @pl.loop(0, jnp.maximum(heads, delay + 2 * half))
+        def _(s):
+            at = s - delay
+
+            @pl.when(jnp.logical_and(at >= 0, at < half))
+            def _():
+                pair_relay(at)
+
+            @pl.when(s < heads)
+            def _():
+                intra(lax.rem(s + y * half, heads))
+
+            @pl.when(jnp.logical_and(at >= OWN_LAG, at < half + OWN_LAG))
+            def _():
+                i = at - OWN_LAG
+                apply_prefix(y * half + i, z_in[i] + jnp.where(y == 0, 0.0, f_in[i]))
+
+            @pl.when(jnp.logical_and(at >= half, at < 2 * half))
+            def _():
+                i = at - half
+                mate_copy(i).wait_recv()
+                apply_prefix((1 - y) * half + i, b_in[i])
+
+        @pl.loop(0, half)
+        def _(i):
+            raw_copy(i).wait_send()
+            mate_copy(i).wait_send()
+
+            @pl.when(up)
+            def _():
+                z_copy(i).wait_send()
 
     pltpu.make_async_copy(gain_hbm, gain_ref, gain_sem).wait()
-    delay = z * STEPS_PER_HOP
-
-    @pl.loop(0, heads + delay + LAG)
-    def _(s):
-        @pl.when(jnp.logical_and(z > 0, jnp.logical_and(s >= delay, s < delay + heads)))
-        def _():
-            relay(s - delay)
-
-        @pl.when(s < heads)
-        def _():
-            intra(s)
-
-        @pl.when(s >= delay + LAG)
-        def _():
-            finalize(s - delay - LAG)
+    if ny == 2 and heads % 2 == 0:
+        run_pairs()
+    else:
+        run_chains()
 
     sums[...] = jnp.sum(jnp.transpose(squares[...]), axis=0, keepdims=True)
     for d in range(1, n_tp):
@@ -219,20 +336,6 @@
 
     for d in range(1, n_tp):
         sum_copy(d).wait_send()
-
-    @pl.loop(0, heads)
-    def _(h):
-        @pl.when(up)
-        def _():
-            z_copy(h).wait_send()
-
-        @pl.when(right)
-        def _():
-            f_copy(h).wait_send()
-
-        @pl.when(left)
-        def _():
-            b_copy(h).wait_send()
 
 
 def norm_kernel(gated_ref, scale_ref, out_hbm, tiles, sems):

time: 46.9 us -> 41.5 us (0.88)
  Pallas kernels: 46.8 us -> 41.4 us
    pallas_call x1, Pallas kernels: 44.6 us -> 39.2 us  [on_device(): pl.pallas_call(functools.partial(attention_kernel, n_ctx, n_tp), out_shap...]
where the time goes in v3:
time: 41.5 us; the launch traced here: 41.4 us
  Pallas kernels  41.4 us (100%)
    pallas_call x1, Pallas kernels, on_device(): pl.pallas_call(functools.partial(attention_kernel, n_ctx, n_tp), out_shap...  39.2 us
    pallas_call x1, Pallas kernels, on_device(): pl.pallas_call(norm_kernel, out_shape=jax.ShapeDtypeStruct((rows, width),...  2.2 us

profile of v3, /device:TPU:25, one launch (start us, length us, event | category | flops | bytes accessed | tf_op | source)
XLA Modules:
  0.0 41.4 jit_solution(11884323781631592569)
XLA Ops:
  0.0 39.2 %attention.1 = (f32[16,1024,128]{2,1,0:T(8,128)S(1)}, f32[1024,128]{1,0:T(8,128)S(1)}) custom-call(bf16[1024,2048]{1,0:T(8,128)(2,1)} %q_hbm.1, bf16[1024,2048]{1,0:T(8,128)(2,1)} %k_hbm.1, bf16[1024,2048]{1,0:T(8,128)(2,1)} %v_hbm.1, bf16[1024,2048]{1,0:T(8,128)(2,1)} %g_hbm.1, f32[16,1,128]{2,1,0:T(1,128)} %bitcast.1), custom_call_target="tpu_custom_call" | custom-call | tf_op jit(solution)/shard_map/attention/pallas_call | solution.py:368
  39.2 2.2 %norm.1 = bf16[1024,2048]{1,0:T(8,128)(2,1)} custom-call(f32[16,1024,128]{2,1,0:T(8,128)S(1)} %get-tuple-element.7.gated_ref, f32[1024,128]{1,0:T(8,128)S(1)} %get-tuple-element.8.scale_ref), custom_call_target="tpu_custom_call" | custom-call | tf_op jit(solution)/shard_map/norm/pallas_call | solution.py:392
